TPU v7x, 32 devices: a whole 2x2x4 slice. The times are simulated.
32 devices in a mesh: row: 8 (over y, x, core), col: 4 (over z).
Axes of the slice: x: 2, y: 2, z: 4, core: 2. Of those that a mesh axis runs over, the one named last changes fastest.
Arguments:
- mode_block: float32 [32768, 256], P(('row', 'col')), may hold values from -80 to 80
- k_blocks: float32 [256, 3, 128, 128], P(('row', 'col')), may hold values from -1 to 9
- block_cols: int32 [256, 3], P(('row', 'col')), may hold values from 0 to 255, as said below
- panel_node: int32 [4096], replicated, may hold values from 0 to 32767, as said below
- added_mass: bfloat16 [4096, 4096], P('row', 'col'), may hold values from -0.125 to 0.125
- low_edge: int32 [256], replicated, may hold values from 4 to 8
- high_edge: int32 [256], replicated, may hold values from 40 to 56
Outputs:
- filtered: float32 [32768, 256], P(('row', 'col'))
Inputs may be any that keep to these rules, and one draw needn't show every extreme that they name: `panel_node`: distinct shell rows. Cut the panels into 32 aligned blocks of 128; in each block at most 8 panels lie on the 1024 rows of one shell device (rows d * 1024 to (d + 1) * 1024 - 1), exactly 8 for some device, and the panels of a block on one device are consecutive. `block_cols`: row i holds i first, then two different block rows among i - 2 to i + 2 other than i.
All inputs are finite; a program needn't handle non-finite values.
Results may differ from a plain program's by a relative error of at most 0.0015.
Values may be sent and summed in bfloat16 or wider, within the bound.
A program may use at most 64 MiB of HBM per device.

v0:
```python
import jax
import jax.numpy as jnp
from jax import lax
from jax.sharding import PartitionSpec as P

DEGREE = 3
OUTER = 2


def with_halo(block, sides, width):
    for axis, dim in sides:
        count = lax.axis_size(axis)
        forward = [(i, i + 1) for i in range(count - 1)]
        backward = [(target, source) for source, target in forward]
        low = lax.ppermute(
            lax.slice_in_dim(block, block.shape[dim] - width, None, axis=dim), axis, forward
        )
        high = lax.ppermute(lax.slice_in_dim(block, 0, width, axis=dim), axis, backward)
        block = jnp.concatenate([low, block, high], axis=dim)
    return block


def body(mode_block, k_blocks, block_cols, panel_node, added_mass, low_edge, high_edge):
    n_row = lax.axis_size("row")
    n_col = lax.axis_size("col")
    devices = n_row * n_col
    my_row = lax.axis_index("row")
    my_col = lax.axis_index("col")
    linear = my_row * n_col + my_col
    rows_dev = mode_block.shape[0]
    mode_width = mode_block.shape[1]
    block_size = k_blocks.shape[2]
    blocks_dev = rows_dev // block_size
    panel_count = panel_node.shape[0]
    per_block = panel_count // devices
    slot_count = 2 * ((per_block + devices - 1) // devices)
    flat_total = devices * slot_count
    panel_rows = panel_node.reshape(devices, per_block)
    source = panel_rows // rows_dev
    within = jnp.arange(per_block)
    earlier = within[None, :] < within[:, None]
    same_source = source[:, :, None] == source[:, None, :]
    slot_rank = jnp.sum((same_source & earlier[None, :, :]).astype(jnp.int32), axis=2)
    block_ids = jnp.arange(devices)[:, None]
    target = block_ids % n_row * n_col + block_ids // n_row
    owned = source == linear
    local_row = panel_rows - linear * rows_dev
    send_flat = jnp.where(owned, target * slot_count + slot_rank, flat_total)
    send_index = jnp.full((flat_total,), rows_dev, dtype=jnp.int32)
    send_index = send_index.at[send_flat.reshape(-1)].set(local_row.reshape(-1), mode="drop")
    return_rows = jnp.where(owned, local_row, rows_dev)
    return_index = jnp.full((rows_dev,), flat_total, dtype=jnp.int32)
    return_index = return_index.at[return_rows.reshape(-1)].set(
        (block_ids * slot_count + slot_rank).reshape(-1), mode="drop"
    )
    in_block = my_col * n_row + my_row
    in_source = lax.dynamic_index_in_dim(source, in_block, 0, keepdims=False)
    in_slot = lax.dynamic_index_in_dim(slot_rank, in_block, 0, keepdims=False)
    in_flat = in_source * slot_count + in_slot
    out_source = lax.dynamic_index_in_dim(source, linear, 0, keepdims=False)
    out_slot = lax.dynamic_index_in_dim(slot_rank, linear, 0, keepdims=False)
    out_index = jnp.full((flat_total,), per_block, dtype=jnp.int32)
    out_index = out_index.at[out_source * slot_count + out_slot].set(within)
    row_source = lax.dynamic_slice_in_dim(source, my_row * n_col, n_col, 0)
    row_slot = lax.dynamic_slice_in_dim(slot_rank, my_row * n_col, n_col, 0)
    row_flat = (
        row_source * (n_col * slot_count) + jnp.arange(n_col)[:, None] * slot_count + row_slot
    )
    part_index = jnp.full((devices * n_col * slot_count,), n_col * per_block, dtype=jnp.int32)
    part_index = part_index.at[row_flat.reshape(-1)].set(jnp.arange(n_col * per_block))
    local_cols = block_cols - (linear * blocks_dev - 2)
    zero_bf = jnp.zeros((1, mode_width), jnp.bfloat16)
    zero_row = jnp.zeros((1, mode_width), jnp.float32)

    def stiffness(vectors):
        padded = with_halo(vectors, ((("row", "col"), 0),), 2 * block_size)
        pieces = padded.reshape(blocks_dev + 4, block_size, mode_width)
        chosen = pieces[local_cols]
        product = jnp.einsum("rkij,rkjn->rin", k_blocks, chosen, precision=lax.Precision.HIGHEST)
        return product.reshape(rows_dev, mode_width)

    def accumulate(arrived_piece):
        return jnp.dot(added_mass, arrived_piece, preferred_element_type=jnp.float32)

    def fluid_loads(vectors):
        rounded = jnp.concatenate([vectors.astype(jnp.bfloat16), zero_bf], axis=0)
        outgoing = rounded[send_index]
        arrived = lax.all_to_all(
            outgoing.reshape(devices, slot_count, mode_width),
            ("row", "col"),
            split_axis=0,
            concat_axis=0,
            tiled=True,
        )
        arrived = arrived.reshape(flat_total, mode_width)
        wetted = arrived[in_flat]
        partial_value = accumulate(lax.all_gather(wetted, "row", axis=0, tiled=True))
        pressure = lax.psum_scatter(partial_value, "col", scatter_dimension=0, tiled=True)
        padded_press = jnp.concatenate([pressure, zero_row], axis=0)
        sending = padded_press[out_index].reshape(devices, slot_count, mode_width)
        summed = lax.all_to_all(
            sending, ("row", "col"), split_axis=0, concat_axis=0, tiled=True
        ).reshape(flat_total, mode_width)
        padded_sum = jnp.concatenate([summed, zero_row], axis=0)
        return padded_sum[return_index]

    def operate(vectors):
        return stiffness(vectors) + fluid_loads(vectors)

    lower = low_edge.astype(jnp.float32) * 0.25
    upper = high_edge.astype(jnp.float32) * 0.25
    centre = 0.5 * (upper + lower)
    radius = 0.5 * (upper - lower)
    total_rows = rows_dev * devices
    current = mode_block
    for outer_no in range(OUTER):
        previous = current
        current = (operate(current) - centre * current) / radius
        for degree_no in range(DEGREE - 1):
            following = 2.0 * (operate(current) - centre * current) / radius - previous
            previous = current
            current = following
        squares = lax.psum(jnp.sum(current * current, axis=0), ("row", "col"))
        current = current / jnp.sqrt(squares / total_rows + 1e-06)
    return current


def solution(mesh):
    placed = (
        P(("row", "col"), None),
        P(("row", "col"), None, None, None),
        P(("row", "col"), None),
        P(),
        P("row", "col"),
        P(),
        P(),
    )
    return jax.shard_map(
        body, mesh=mesh, in_specs=placed, out_specs=P(("row", "col"), None), check_vma=False
    )
```

profile of v0, /device:TPU:0, one launch (start us, length us, event | category | flops | bytes accessed | tf_op | source)
XLA Modules:
  0.0 587.2 jit_solution(11731140511086322295)
XLA Ops:
  9.5 15.5 %scatter_custom_fusion = s32[256]{0:T(256)S(1)} fusion(s32[4096]{0:T(1024)S(1)} %get-tuple-element.35, s32[4096]{0:T(1024)S(1)} %get-tuple-element.20, s32[]{:T(128)} %constant.94.clone.1), kind=kCustom, calls=%fused_computation.139 | custom fusion | bytes 1028 | tf_op jit(solution)/shard_map/scatter | solution.py:50
  28.2 7.3 %all-to-all-start = ((bf16[32,8,256]{2,1,0:T(8,128)(2,1)}), bf16[32,8,256]{2,1,0:T(8,128)(2,1)S(1)}, u32[]{:S(2)}, u32[]{:S(2)}) async-start(bf16[32,8,256]{2,1,0:T(8,128)(2,1)} %bitcast.8), calls=%async_computation | async-start | bytes 262144 | tf_op jit(solution)/shard_map/all_to_all | solution.py:88
  44.8 13.9 %all-gather = bf16[1024,256]{1,0:T(8,128)(2,1)S(1)} all-gather(bf16[128,256]{1,0:T(8,128)(2,1)S(1)} %gather_fusion.2), channel_id=2, replica_groups=mesh['row'=8,'col'=4] {'row'}, dimensions={0}, use_global_device_ids=true | all-gather | bytes 589824 | tf_op jit(solution)/shard_map/all_gather | solution.py:97
  60.3 15.5 %scatter_custom_fusion.2 = s32[1024]{0:T(1024)S(1)} fusion(s32[4096]{0:T(1024)S(1)} %get-tuple-element.19, s32[4096]{0:T(1024)S(1)} %add_bitcast_fusion, s32[]{:T(128)} %constant.101.clone.1), kind=kCustom, calls=%fused_computation.110 | custom fusion | bytes 4100 | tf_op jit(solution)/shard_map/scatter | solution.py:53
  91.9 5.1 fusion.59
  106.0 14.0 %all_to_all.60 = bf16[32,8,256]{2,1,0:T(8,128)(2,1)S(1)} all-to-all(bf16[32,8,256]{2,1,0:T(8,128)(2,1)S(1)} %bitcast.215), channel_id=1, replica_groups=mesh['row'=8,'col'=4] {'row','col'}, dimensions={0} | all-to-all | bytes 262144 | tf_op jit(solution)/shard_map/all_to_all | solution.py:88
  120.8 9.6 %all-gather.1 = bf16[1024,256]{1,0:T(8,128)(2,1)S(1)} all-gather(bf16[128,256]{1,0:T(8,128)(2,1)S(1)} %gather_fusion.7), channel_id=3, replica_groups=mesh['row'=8,'col'=4] {'row'}, dimensions={0}, use_global_device_ids=true | all-gather | bytes 589824 | tf_op jit(solution)/shard_map/all_gather | solution.py:97
  136.7 20.1 %reduce-scatter.9.cloned.1.call-done = f32[128,256]{0,1:T(8,128)} async-done(((f32[512,256]{0,1:T(8,128)}), f32[128,256]{0,1:T(8,128)}) %reduce-scatter.9.cloned.1.call-update) | async-done | bytes 131088 | tf_op jit(solution)/shard_map/reduce_scatter | solution.py:98
  170.6 5.1 fusion.60
  185.1 14.0 %all_to_all.61 = bf16[32,8,256]{2,1,0:T(8,128)(2,1)S(1)} all-to-all(bf16[32,8,256]{2,1,0:T(8,128)(2,1)S(1)} %bitcast.216), channel_id=1, replica_groups=mesh['row'=8,'col'=4] {'row','col'}, dimensions={0} | all-to-all | bytes 262144 | tf_op jit(solution)/shard_map/all_to_all | solution.py:88
  200.0 9.1 %all-gather.2 = bf16[1024,256]{1,0:T(8,128)(2,1)S(1)} all-gather(bf16[128,256]{1,0:T(8,128)(2,1)S(1)} %gather_fusion.12), channel_id=4, replica_groups=mesh['row'=8,'col'=4] {'row'}, dimensions={0}, use_global_device_ids=true | all-gather | bytes 589824 | tf_op jit(solution)/shard_map/all_gather | solution.py:97
  215.4 20.1 %reduce-scatter.11.cloned.1.call-done = f32[128,256]{0,1:T(8,128)} async-done(((f32[512,256]{0,1:T(8,128)}), f32[128,256]{0,1:T(8,128)}) %reduce-scatter.11.cloned.1.call-update) | async-done | bytes 131088 | tf_op jit(solution)/shard_map/reduce_scatter | solution.py:98
  262.7 40.4 %psum.14 = f32[256]{0:T(256)S(1)} all-reduce(f32[256]{0:T(256)S(1)} %get-tuple-element.13), channel_id=1, replica_groups=mesh['row'=8,'col'=4] {'row','col'}, use_global_device_ids=true, to_apply=%region_8.9 | all-reduce | flops 256 | bytes 2048 | tf_op jit(solution)/shard_map/psum | solution.py:123
  306.6 12.7 %all_to_all.62 = bf16[32,8,256]{2,1,0:T(8,128)(2,1)S(1)} all-to-all(bf16[32,8,256]{2,1,0:T(8,128)(2,1)S(1)} %bitcast.217), channel_id=1, replica_groups=mesh['row'=8,'col'=4] {'row','col'}, dimensions={0} | all-to-all | bytes 262144 | tf_op jit(solution)/shard_map/all_to_all | solution.py:88
  320.1 9.1 %all-gather.3 = bf16[1024,256]{1,0:T(8,128)(2,1)S(1)} all-gather(bf16[128,256]{1,0:T(8,128)(2,1)S(1)} %gather_fusion.17), channel_id=5, replica_groups=mesh['row'=8,'col'=4] {'row'}, dimensions={0}, use_global_device_ids=true | all-gather | bytes 589824 | tf_op jit(solution)/shard_map/all_gather | solution.py:97
  335.5 20.1 %reduce-scatter.13.cloned.1.call-done = f32[128,256]{0,1:T(8,128)} async-done(((f32[512,256]{0,1:T(8,128)}), f32[128,256]{0,1:T(8,128)}) %reduce-scatter.13.cloned.1.call-update) | async-done | bytes 131088 | tf_op jit(solution)/shard_map/reduce_scatter | solution.py:98
  369.4 5.1 fusion.62
  383.5 14.0 %all_to_all.63 = bf16[32,8,256]{2,1,0:T(8,128)(2,1)S(1)} all-to-all(bf16[32,8,256]{2,1,0:T(8,128)(2,1)S(1)} %bitcast.218), channel_id=1, replica_groups=mesh['row'=8,'col'=4] {'row','col'}, dimensions={0} | all-to-all | bytes 262144 | tf_op jit(solution)/shard_map/all_to_all | solution.py:88
  398.4 9.3 %all-gather.4 = bf16[1024,256]{1,0:T(8,128)(2,1)S(1)} all-gather(bf16[128,256]{1,0:T(8,128)(2,1)S(1)} %gather_fusion.22), channel_id=6, replica_groups=mesh['row'=8,'col'=4] {'row'}, dimensions={0}, use_global_device_ids=true | all-gather | bytes 589824 | tf_op jit(solution)/shard_map/all_gather | solution.py:97
  414.0 20.1 %reduce-scatter.15.cloned.1.call-done = f32[128,256]{0,1:T(8,128)} async-done(((f32[512,256]{0,1:T(8,128)}), f32[128,256]{0,1:T(8,128)}) %reduce-scatter.15.cloned.1.call-update) | async-done | bytes 131088 | tf_op jit(solution)/shard_map/reduce_scatter | solution.py:98
  462.3 14.0 %all_to_all.64 = bf16[32,8,256]{2,1,0:T(8,128)(2,1)S(1)} all-to-all(bf16[32,8,256]{2,1,0:T(8,128)(2,1)S(1)} %bitcast.214), channel_id=1, replica_groups=mesh['row'=8,'col'=4] {'row','col'}, dimensions={0} | all-to-all | bytes 262144 | tf_op jit(solution)/shard_map/all_to_all | solution.py:88
  477.2 9.1 %all-gather.5 = bf16[1024,256]{1,0:T(8,128)(2,1)S(1)} all-gather(bf16[128,256]{1,0:T(8,128)(2,1)S(1)} %gather_fusion.27), channel_id=7, replica_groups=mesh['row'=8,'col'=4] {'row'}, dimensions={0}, use_global_device_ids=true | all-gather | bytes 589824 | tf_op jit(solution)/shard_map/all_gather | solution.py:97
  491.8 21.1 %reduce-scatter.17.cloned.1.call-done = f32[128,256]{0,1:T(8,128)} async-done(((f32[512,256]{0,1:T(8,128)}), f32[128,256]{0,1:T(8,128)}) %reduce-scatter.17.cloned.1.call-update) | async-done | bytes 131088 | tf_op jit(solution)/shard_map/reduce_scatter | solution.py:98
  538.5 40.5 %psum.15 = f32[256]{0:T(256)S(1)} all-reduce(f32[256]{0:T(256)S(1)} %get-tuple-element.5), channel_id=1, replica_groups=mesh['row'=8,'col'=4] {'row','col'}, use_global_device_ids=true, to_apply=%region_13.14 | all-reduce | flops 256 | bytes 2048 | tf_op jit(solution)/shard_map/psum | solution.py:123
  (167 shorter events, 207.8 us)
Async XLA Ops:
  28.2 15.7 %all-to-all-start = ((bf16[32,8,256]{2,1,0:T(8,128)(2,1)}), bf16[32,8,256]{2,1,0:T(8,128)(2,1)S(1)}, u32[]{:S(2)}, u32[]{:S(2)}) async-start(bf16[32,8,256]{2,1,0:T(8,128)(2,1)} %bitcast.8), calls=%async_computation | async-start | bytes 262144 | tf_op jit(solution)/shard_map/all_to_all | solution.py:88
  35.5 44.4 %reduce-scatter.7.cloned.1.call-start = ((), (), s32[]{:S(2)}) async-start(), calls=%async_computation.18 | async-start | bytes 655360 | tf_op jit(solution)/shard_map/reduce_scatter | solution.py:98
  37.4 48.1 %collective-permute-start = (f32[256,256]{1,0:T(8,128)}, f32[256,256]{1,0:T(8,128)S(1)}, u32[]{:S(2)}, u32[]{:S(2)}) collective-permute-start(f32[256,256]{1,0:T(8,128)} %get-tuple-element.31), channel_id=1, source_target_pairs={{0,1},{1,2},{2,3},{3,4},{4,5},{5,6},{6,7},{7,8},{8,9},{9,10},{10,1... | collective-permute-start | bytes 786440 | tf_op jit(solution)/shard_map/ppermute | solution.py:15
  41.1 44.4 %collective-permute-start.1 = (f32[256,256]{1,0:T(8,128)}, f32[256,256]{1,0:T(8,128)}, u32[]{:S(2)}, u32[]{:S(2)}) collective-permute-start(f32[256,256]{1,0:T(8,128)} %get-tuple-element.32), channel_id=1, source_target_pairs={{1,0},{2,1},{3,2},{4,3},{5,4},{6,5},{7,6},{8,7},{9,8},{10,9},{11,1... | collective-permute-start | bytes 786440 | tf_op jit(solution)/shard_map/ppermute | solution.py:18
  85.5 71.3 %reduce-scatter.9.cloned.1.call-start = ((), (), s32[]{:S(2)}) async-start(), calls=%async_computation.19 | async-start | bytes 655360 | tf_op jit(solution)/shard_map/reduce_scatter | solution.py:98
  133.6 30.5 %collective-permute-start.2 = (f32[256,256]{1,0:T(8,128)}, f32[256,256]{1,0:T(8,128)S(1)}, u32[]{:S(2)}, u32[]{:S(2)}) collective-permute-start(f32[256,256]{1,0:T(8,128)} %get-tuple-element.29), channel_id=1, source_target_pairs={{0,1},{1,2},{2,3},{3,4},{4,5},{5,6},{6,7},{7,8},{8,9},{9,10},{10,1... | collective-permute-start | bytes 786440 | tf_op jit(solution)/shard_map/ppermute | solution.py:15
  135.4 28.8 %collective-permute-start.3 = (f32[256,256]{1,0:T(8,128)}, f32[256,256]{1,0:T(8,128)}, u32[]{:S(2)}, u32[]{:S(2)}) collective-permute-start(f32[256,256]{1,0:T(8,128)} %get-tuple-element.30), channel_id=1, source_target_pairs={{1,0},{2,1},{3,2},{4,3},{5,4},{6,5},{7,6},{8,7},{9,8},{10,9},{11,1... | collective-permute-start | bytes 786440 | tf_op jit(solution)/shard_map/ppermute | solution.py:18
  159.5 16.3 %all-to-all-start.3 = ((f32[32,8,256]{2,1,0:T(8,128)}), f32[32,8,256]{2,1,0:T(8,128)S(1)}, u32[]{:S(2)}, u32[]{:S(2)}) async-start(f32[32,8,256]{2,1,0:T(8,128)} %bitcast.27), calls=%async_computation.5 | async-start | bytes 524288 | tf_op jit(solution)/shard_map/all_to_all | solution.py:101
  164.1 71.3 %reduce-scatter.11.cloned.1.call-start = ((), (), s32[]{:S(2)}) async-start(), calls=%async_computation.20 | async-start | bytes 655360 | tf_op jit(solution)/shard_map/reduce_scatter | solution.py:98
  212.3 30.7 %collective-permute-start.4 = (f32[256,256]{1,0:T(8,128)}, f32[256,256]{1,0:T(8,128)S(1)}, u32[]{:S(2)}, u32[]{:S(2)}) collective-permute-start(f32[256,256]{1,0:T(8,128)} %get-tuple-element.27), channel_id=1, source_target_pairs={{0,1},{1,2},{2,3},{3,4},{4,5},{5,6},{6,7},{7,8},{8,9},{9,10},{10,1... | collective-permute-start | bytes 786440 | tf_op jit(solution)/shard_map/ppermute | solution.py:15
  214.1 28.9 %collective-permute-start.5 = (f32[256,256]{1,0:T(8,128)}, f32[256,256]{1,0:T(8,128)}, u32[]{:S(2)}, u32[]{:S(2)}) collective-permute-start(f32[256,256]{1,0:T(8,128)} %get-tuple-element.28), channel_id=1, source_target_pairs={{1,0},{2,1},{3,2},{4,3},{5,4},{6,5},{7,6},{8,7},{9,8},{10,9},{11,1... | collective-permute-start | bytes 786440 | tf_op jit(solution)/shard_map/ppermute | solution.py:18
  238.2 16.4 %all-to-all-start.5 = ((f32[32,8,256]{2,1,0:T(8,128)}), f32[32,8,256]{2,1,0:T(8,128)S(1)}, u32[]{:S(2)}, u32[]{:S(2)}) async-start(f32[32,8,256]{2,1,0:T(8,128)} %bitcast.38), calls=%async_computation.8 | async-start | bytes 524288 | tf_op jit(solution)/shard_map/all_to_all | solution.py:101
  242.8 112.8 %reduce-scatter.13.cloned.1.call-start = ((), (), s32[]{:S(2)}) async-start(), calls=%async_computation.21 | async-start | bytes 655360 | tf_op jit(solution)/shard_map/reduce_scatter | solution.py:98
  332.5 30.5 %collective-permute-start.6 = (f32[256,256]{1,0:T(8,128)}, f32[256,256]{1,0:T(8,128)S(1)}, u32[]{:S(2)}, u32[]{:S(2)}) collective-permute-start(f32[256,256]{1,0:T(8,128)} %get-tuple-element.25), channel_id=1, source_target_pairs={{0,1},{1,2},{2,3},{3,4},{4,5},{5,6},{6,7},{7,8},{8,9},{9,10},{10,1... | collective-permute-start | bytes 786440 | tf_op jit(solution)/shard_map/ppermute | solution.py:15
  334.2 28.8 %collective-permute-start.7 = (f32[256,256]{1,0:T(8,128)}, f32[256,256]{1,0:T(8,128)}, u32[]{:S(2)}, u32[]{:S(2)}) collective-permute-start(f32[256,256]{1,0:T(8,128)} %get-tuple-element.26), channel_id=1, source_target_pairs={{1,0},{2,1},{3,2},{4,3},{5,4},{6,5},{7,6},{8,7},{9,8},{10,9},{11,1... | collective-permute-start | bytes 786440 | tf_op jit(solution)/shard_map/ppermute | solution.py:18
  358.3 16.2 %all-to-all-start.7 = ((f32[32,8,256]{2,1,0:T(8,128)}), f32[32,8,256]{2,1,0:T(8,128)S(1)}, u32[]{:S(2)}, u32[]{:S(2)}) async-start(f32[32,8,256]{2,1,0:T(8,128)} %bitcast.49), calls=%async_computation.11 | async-start | bytes 524288 | tf_op jit(solution)/shard_map/all_to_all | solution.py:101
  362.9 71.1 %reduce-scatter.15.cloned.1.call-start = ((), (), s32[]{:S(2)}) async-start(), calls=%async_computation.22 | async-start | bytes 655360 | tf_op jit(solution)/shard_map/reduce_scatter | solution.py:98
  410.9 30.5 %collective-permute-start.8 = (f32[256,256]{1,0:T(8,128)}, f32[256,256]{1,0:T(8,128)S(1)}, u32[]{:S(2)}, u32[]{:S(2)}) collective-permute-start(f32[256,256]{1,0:T(8,128)} %get-tuple-element.23), channel_id=1, source_target_pairs={{0,1},{1,2},{2,3},{3,4},{4,5},{5,6},{6,7},{7,8},{8,9},{9,10},{10,1... | collective-permute-start | bytes 786440 | tf_op jit(solution)/shard_map/ppermute | solution.py:15
  412.7 28.7 %collective-permute-start.9 = (f32[256,256]{1,0:T(8,128)}, f32[256,256]{1,0:T(8,128)}, u32[]{:S(2)}, u32[]{:S(2)}) collective-permute-start(f32[256,256]{1,0:T(8,128)} %get-tuple-element.24), channel_id=1, source_target_pairs={{1,0},{2,1},{3,2},{4,3},{5,4},{6,5},{7,6},{8,7},{9,8},{10,9},{11,1... | collective-permute-start | bytes 786440 | tf_op jit(solution)/shard_map/ppermute | solution.py:18
  436.7 16.2 %all-to-all-start.9 = ((f32[32,8,256]{2,1,0:T(8,128)}), f32[32,8,256]{2,1,0:T(8,128)S(1)}, u32[]{:S(2)}, u32[]{:S(2)}) async-start(f32[32,8,256]{2,1,0:T(8,128)} %bitcast.60), calls=%async_computation.14 | async-start | bytes 524288 | tf_op jit(solution)/shard_map/all_to_all | solution.py:101
  441.4 71.5 %reduce-scatter.17.cloned.1.call-start = ((), (), s32[]{:S(2)}) async-start(), calls=%async_computation.23 | async-start | bytes 655360 | tf_op jit(solution)/shard_map/reduce_scatter | solution.py:98
  488.7 31.2 %collective-permute-start.10 = (f32[256,256]{1,0:T(8,128)S(1)}, f32[256,256]{1,0:T(8,128)S(1)}, u32[]{:S(2)}, u32[]{:S(2)}) collective-permute-start(f32[256,256]{1,0:T(8,128)S(1)} %get-tuple-element.21), channel_id=1, source_target_pairs={{0,1},{1,2},{2,3},{3,4},{4,5},{5,6},{6,7},{7,8},{8,9},{9,10},{10,1... | collective-permute-start | bytes 786440 | tf_op jit(solution)/shard_map/ppermute | solution.py:15
  490.5 29.4 %collective-permute-start.11 = (f32[256,256]{1,0:T(8,128)S(1)}, f32[256,256]{1,0:T(8,128)S(1)}, u32[]{:S(2)}, u32[]{:S(2)}) collective-permute-start(f32[256,256]{1,0:T(8,128)S(1)} %get-tuple-element.22), channel_id=1, source_target_pairs={{1,0},{2,1},{3,2},{4,3},{5,4},{6,5},{7,6},{8,7},{9,8},{10,9},{11,1... | collective-permute-start | bytes 786440 | tf_op jit(solution)/shard_map/ppermute | solution.py:18
  515.5 15.7 %all-to-all-start.11 = ((f32[32,8,256]{2,1,0:T(8,128)}), f32[32,8,256]{2,1,0:T(8,128)S(1)}, u32[]{:S(2)}, u32[]{:S(2)}) async-start(f32[32,8,256]{2,1,0:T(8,128)} %bitcast.71), calls=%async_computation.17 | async-start | bytes 524288 | tf_op jit(solution)/shard_map/all_to_all | solution.py:101
  (6 other events, 180.0 us)
Sparse Core Ops, SparseCore 0:
  60.1 19.7 reduce-scatter.6
  131.9 24.8 reduce-scatter.8
  210.5 24.8 reduce-scatter.10
  330.7 24.8 reduce-scatter.12
  409.1 24.8 reduce-scatter.14
  487.7 25.0 reduce-scatter.16
where the time goes:
time: 597 us; the launch traced here: 587 us
  blocking collectives  210 us (35%)
  local copies, waits for them, and re-layouts  123 us (21%)
  waiting for transfers between devices  106 us (18%)
  starting transfers between devices  53.7 us (9%)
  other arithmetic  42.1 us (7%)
  matrix products  38.6 us (6%)
  between operations  14.5 us (2%)
    reduce_scatter x6, waiting for transfers between devices, fluid_loads(): lax.psum_scatter(partial_value, 'col', scatter_dimension=0, tiled=True)  105 us
    psum x2, blocking collectives, body(): squares = lax.psum(jnp.sum(current * current, axis=0), ('row', 'col'))  80.9 us
    all_to_all x5, blocking collectives, fluid_loads(): lax.all_to_all(outgoing.reshape(devices, slot_count, mode_width), ('row',...  68.7 us
    all_gather x6, blocking collectives, fluid_loads(): lax.all_gather(wetted, 'row', axis=0, tiled=True)  60.2 us
    dot_general x6, matrix products, stiffness(): jnp.einsum('rkij,rkjn->rin', k_blocks, chosen, precision=lax.Precision.HI...  30.9 us
    gather x6, local copies, waits for them, and re-layouts, fluid_loads(): return padded_sum[return_index]  28.2 us
    all_to_all x6, starting transfers between devices, fluid_loads(): lax.all_to_all(sending, ('row', 'col'), split_axis=0, concat_axis=0, tile...  25.7 us
    gather x6, local copies, waits for them, and re-layouts, stiffness(): chosen = pieces[local_cols]  22.7 us
  transfers between devices with their start and end apart: 25, of which 7 were waited for; matrix products, arithmetic and copies ran while one was open for 20% of the time, Pallas kernels for 0%

commit v1 on v0

--- a/solution.py
+++ b/solution.py
@@ -1,3 +1,4 @@
+import functools
 import jax
 import jax.numpy as jnp
 from jax import lax
@@ -5,6 +6,14 @@
 
 DEGREE = 3
 OUTER = 2
+
+
+def mix_tokens(payload, group_axis):
+    piece_out = jnp.sum(jax.lax.all_gather(payload, group_axis), axis=0)
+    return piece_out
+
+
+_draw_wires = functools.partial(mix_tokens, group_axis=("row", "col"))
 
 
 def with_halo(block, sides, width):
@@ -120,7 +129,7 @@
             following = 2.0 * (operate(current) - centre * current) / radius - previous
             previous = current
             current = following
-        squares = lax.psum(jnp.sum(current * current, axis=0), ("row", "col"))
+        squares = _draw_wires(jnp.sum(current * current, axis=0))
         current = current / jnp.sqrt(squares / total_rows + 1e-06)
     return current
 

time: 597 us -> 651 us (1.090)
  blocking collectives: 210 us -> 264 us
    all_gather x0 -> x2, blocking collectives: none -> 138 us  [mix_tokens(): piece_out = jnp.sum(jax.lax.all_gather(payload, group_axis), axis=0)]
    psum x2 -> x0, blocking collectives: 80.9 us -> none  [body(): squares = lax.psum(jnp.sum(current * current, axis=0), ('row', 'col'))]
  transfers between devices with their start and end apart: 25 -> 25, of which waited for: 7 -> 7; matrix products, arithmetic and copies ran while one was open for 20% -> 18% of each run, Pallas kernels for 0% -> 0%
where the time goes in v1:
time: 651 us; the launch traced here: 641 us
  blocking collectives  264 us (41%)
  local copies, waits for them, and re-layouts  123 us (19%)
  waiting for transfers between devices  106 us (16%)
  starting transfers between devices  53.7 us (8%)
  other arithmetic  42.2 us (6%)
  matrix products  38.6 us (6%)
  between operations  14.4 us (2%)
    all_gather x2, blocking collectives, mix_tokens(): piece_out = jnp.sum(jax.lax.all_gather(payload, group_axis), axis=0)  138 us
    reduce_scatter x6, waiting for transfers between devices, fluid_loads(): lax.psum_scatter(partial_value, 'col', scatter_dimension=0, tiled=True)  105 us
    all_to_all x5, blocking collectives, fluid_loads(): lax.all_to_all(outgoing.reshape(devices, slot_count, mode_width), ('row',...  66.2 us
    all_gather x6, blocking collectives, fluid_loads(): lax.all_gather(wetted, 'row', axis=0, tiled=True)  59.9 us
    dot_general x6, matrix products, stiffness(): jnp.einsum('rkij,rkjn->rin', k_blocks, chosen, precision=lax.Precision.HI...  30.9 us
    gather x6, local copies, waits for them, and re-layouts, fluid_loads(): return padded_sum[return_index]  28.2 us
    all_to_all x6, starting transfers between devices, fluid_loads(): lax.all_to_all(sending, ('row', 'col'), split_axis=0, concat_axis=0, tile...  25.6 us
    gather x6, local copies, waits for them, and re-layouts, stiffness(): chosen = pieces[local_cols]  22.7 us
  transfers between devices with their start and end apart: 25, of which 7 were waited for; matrix products, arithmetic and copies ran while one was open for 18% of the time, Pallas kernels for 0%

profile of v1, /device:TPU:0, one launch (start us, length us, event | category | flops | bytes accessed | tf_op | source)
XLA Modules:
  0.0 641.1 jit_solution(2524085275768204309)
XLA Ops:
  9.5 15.5 %scatter_custom_fusion = s32[256]{0:T(256)S(1)} fusion(s32[4096]{0:T(1024)S(1)} %get-tuple-element.35, s32[4096]{0:T(1024)S(1)} %get-tuple-element.20, s32[]{:T(128)} %constant.94.clone.1), kind=kCustom, calls=%fused_computation.139 | custom fusion | bytes 1028 | tf_op jit(solution)/shard_map/scatter | solution.py:59
  28.2 7.3 %all-to-all-start = ((bf16[32,8,256]{2,1,0:T(8,128)(2,1)}), bf16[32,8,256]{2,1,0:T(8,128)(2,1)S(1)}, u32[]{:S(2)}, u32[]{:S(2)}) async-start(bf16[32,8,256]{2,1,0:T(8,128)(2,1)} %bitcast.8), calls=%async_computation | async-start | bytes 262144 | tf_op jit(solution)/shard_map/all_to_all | solution.py:97
  44.8 13.9 %all-gather = bf16[1024,256]{1,0:T(8,128)(2,1)S(1)} all-gather(bf16[128,256]{1,0:T(8,128)(2,1)S(1)} %gather_fusion.2), channel_id=2, replica_groups=mesh['row'=8,'col'=4] {'row'}, dimensions={0}, use_global_device_ids=true | all-gather | bytes 589824 | tf_op jit(solution)/shard_map/all_gather | solution.py:106
  60.3 15.5 %scatter_custom_fusion.2 = s32[1024]{0:T(1024)S(1)} fusion(s32[4096]{0:T(1024)S(1)} %get-tuple-element.19, s32[4096]{0:T(1024)S(1)} %add_bitcast_fusion, s32[]{:T(128)} %constant.101.clone.1), kind=kCustom, calls=%fused_computation.110 | custom fusion | bytes 4100 | tf_op jit(solution)/shard_map/scatter | solution.py:62
  91.9 5.1 fusion.59
  106.0 14.0 %all_to_all.60 = bf16[32,8,256]{2,1,0:T(8,128)(2,1)S(1)} all-to-all(bf16[32,8,256]{2,1,0:T(8,128)(2,1)S(1)} %bitcast.217), channel_id=1, replica_groups=mesh['row'=8,'col'=4] {'row','col'}, dimensions={0} | all-to-all | bytes 262144 | tf_op jit(solution)/shard_map/all_to_all | solution.py:97
  120.8 9.6 %all-gather.1 = bf16[1024,256]{1,0:T(8,128)(2,1)S(1)} all-gather(bf16[128,256]{1,0:T(8,128)(2,1)S(1)} %gather_fusion.7), channel_id=3, replica_groups=mesh['row'=8,'col'=4] {'row'}, dimensions={0}, use_global_device_ids=true | all-gather | bytes 589824 | tf_op jit(solution)/shard_map/all_gather | solution.py:106
  136.7 20.1 %reduce-scatter.9.cloned.1.call-done = f32[128,256]{0,1:T(8,128)} async-done(((f32[512,256]{0,1:T(8,128)}), f32[128,256]{0,1:T(8,128)}) %reduce-scatter.9.cloned.1.call-update) | async-done | bytes 131088 | tf_op jit(solution)/shard_map/reduce_scatter | solution.py:107
  170.6 5.1 fusion.60
  185.1 14.0 %all_to_all.61 = bf16[32,8,256]{2,1,0:T(8,128)(2,1)S(1)} all-to-all(bf16[32,8,256]{2,1,0:T(8,128)(2,1)S(1)} %bitcast.218), channel_id=1, replica_groups=mesh['row'=8,'col'=4] {'row','col'}, dimensions={0} | all-to-all | bytes 262144 | tf_op jit(solution)/shard_map/all_to_all | solution.py:97
  200.0 9.1 %all-gather.2 = bf16[1024,256]{1,0:T(8,128)(2,1)S(1)} all-gather(bf16[128,256]{1,0:T(8,128)(2,1)S(1)} %gather_fusion.12), channel_id=4, replica_groups=mesh['row'=8,'col'=4] {'row'}, dimensions={0}, use_global_device_ids=true | all-gather | bytes 589824 | tf_op jit(solution)/shard_map/all_gather | solution.py:106
  215.4 20.1 %reduce-scatter.11.cloned.1.call-done = f32[128,256]{0,1:T(8,128)} async-done(((f32[512,256]{0,1:T(8,128)}), f32[128,256]{0,1:T(8,128)}) %reduce-scatter.11.cloned.1.call-update) | async-done | bytes 131088 | tf_op jit(solution)/shard_map/reduce_scatter | solution.py:107
  249.2 5.2 fusion.61
  262.5 68.9 %all-gather.8 = f32[32,1,256]{2,1,0:T(1,128)S(1)} all-gather(f32[1,1,256]{2,1,0:T(1,128)S(1)} %bitcast.222), channel_id=5, replica_groups=mesh['row'=8,'col'=4] {'row','col'}, dimensions={0}, use_global_device_ids=true | all-gather | bytes 33792 | tf_op jit(solution)/shard_map/all_gather | solution.py:12
  335.0 10.1 %all_to_all.62 = bf16[32,8,256]{2,1,0:T(8,128)(2,1)S(1)} all-to-all(bf16[32,8,256]{2,1,0:T(8,128)(2,1)S(1)} %bitcast.219), channel_id=1, replica_groups=mesh['row'=8,'col'=4] {'row','col'}, dimensions={0} | all-to-all | bytes 262144 | tf_op jit(solution)/shard_map/all_to_all | solution.py:97
  345.9 9.1 %all-gather.4 = bf16[1024,256]{1,0:T(8,128)(2,1)S(1)} all-gather(bf16[128,256]{1,0:T(8,128)(2,1)S(1)} %gather_fusion.17), channel_id=6, replica_groups=mesh['row'=8,'col'=4] {'row'}, dimensions={0}, use_global_device_ids=true | all-gather | bytes 589824 | tf_op jit(solution)/shard_map/all_gather | solution.py:106
  361.3 20.1 %reduce-scatter.13.cloned.1.call-done = f32[128,256]{0,1:T(8,128)} async-done(((f32[512,256]{0,1:T(8,128)}), f32[128,256]{0,1:T(8,128)}) %reduce-scatter.13.cloned.1.call-update) | async-done | bytes 131088 | tf_op jit(solution)/shard_map/reduce_scatter | solution.py:107
  409.3 14.0 %all_to_all.63 = bf16[32,8,256]{2,1,0:T(8,128)(2,1)S(1)} all-to-all(bf16[32,8,256]{2,1,0:T(8,128)(2,1)S(1)} %bitcast.220), channel_id=1, replica_groups=mesh['row'=8,'col'=4] {'row','col'}, dimensions={0} | all-to-all | bytes 262144 | tf_op jit(solution)/shard_map/all_to_all | solution.py:97
  424.1 9.1 %all-gather.5 = bf16[1024,256]{1,0:T(8,128)(2,1)S(1)} all-gather(bf16[128,256]{1,0:T(8,128)(2,1)S(1)} %gather_fusion.22), channel_id=7, replica_groups=mesh['row'=8,'col'=4] {'row'}, dimensions={0}, use_global_device_ids=true | all-gather | bytes 589824 | tf_op jit(solution)/shard_map/all_gather | solution.py:106
  439.5 20.1 %reduce-scatter.15.cloned.1.call-done = f32[128,256]{0,1:T(8,128)} async-done(((f32[512,256]{0,1:T(8,128)}), f32[128,256]{0,1:T(8,128)}) %reduce-scatter.15.cloned.1.call-update) | async-done | bytes 131088 | tf_op jit(solution)/shard_map/reduce_scatter | solution.py:107
  488.0 14.0 %all_to_all.64 = bf16[32,8,256]{2,1,0:T(8,128)(2,1)S(1)} all-to-all(bf16[32,8,256]{2,1,0:T(8,128)(2,1)S(1)} %bitcast.216), channel_id=1, replica_groups=mesh['row'=8,'col'=4] {'row','col'}, dimensions={0} | all-to-all | bytes 262144 | tf_op jit(solution)/shard_map/all_to_all | solution.py:97
  502.9 9.1 %all-gather.6 = bf16[1024,256]{1,0:T(8,128)(2,1)S(1)} all-gather(bf16[128,256]{1,0:T(8,128)(2,1)S(1)} %gather_fusion.27), channel_id=8, replica_groups=mesh['row'=8,'col'=4] {'row'}, dimensions={0}, use_global_device_ids=true | all-gather | bytes 589824 | tf_op jit(solution)/shard_map/all_gather | solution.py:106
  517.5 21.1 %reduce-scatter.17.cloned.1.call-done = f32[128,256]{0,1:T(8,128)} async-done(((f32[512,256]{0,1:T(8,128)}), f32[128,256]{0,1:T(8,128)}) %reduce-scatter.17.cloned.1.call-update) | async-done | bytes 131088 | tf_op jit(solution)/shard_map/reduce_scatter | solution.py:107
  564.2 68.7 %all-gather.9 = f32[32,1,256]{2,1,0:T(1,128)S(1)} all-gather(f32[1,1,256]{2,1,0:T(1,128)S(1)} %bitcast.221), channel_id=9, replica_groups=mesh['row'=8,'col'=4] {'row','col'}, dimensions={0}, use_global_device_ids=true | all-gather | bytes 33792 | tf_op jit(solution)/shard_map/all_gather | solution.py:12
  (169 shorter events, 207.9 us)
Async XLA Ops:
  28.2 15.7 %all-to-all-start = ((bf16[32,8,256]{2,1,0:T(8,128)(2,1)}), bf16[32,8,256]{2,1,0:T(8,128)(2,1)S(1)}, u32[]{:S(2)}, u32[]{:S(2)}) async-start(bf16[32,8,256]{2,1,0:T(8,128)(2,1)} %bitcast.8), calls=%async_computation | async-start | bytes 262144 | tf_op jit(solution)/shard_map/all_to_all | solution.py:97
  35.5 44.4 %reduce-scatter.7.cloned.1.call-start = ((), (), s32[]{:S(2)}) async-start(), calls=%async_computation.18 | async-start | bytes 655360 | tf_op jit(solution)/shard_map/reduce_scatter | solution.py:107
  37.4 48.1 %collective-permute-start = (f32[256,256]{1,0:T(8,128)}, f32[256,256]{1,0:T(8,128)S(1)}, u32[]{:S(2)}, u32[]{:S(2)}) collective-permute-start(f32[256,256]{1,0:T(8,128)} %get-tuple-element.31), channel_id=1, source_target_pairs={{0,1},{1,2},{2,3},{3,4},{4,5},{5,6},{6,7},{7,8},{8,9},{9,10},{10,1... | collective-permute-start | bytes 786440 | tf_op jit(solution)/shard_map/ppermute | solution.py:24
  41.1 44.4 %collective-permute-start.1 = (f32[256,256]{1,0:T(8,128)}, f32[256,256]{1,0:T(8,128)}, u32[]{:S(2)}, u32[]{:S(2)}) collective-permute-start(f32[256,256]{1,0:T(8,128)} %get-tuple-element.32), channel_id=1, source_target_pairs={{1,0},{2,1},{3,2},{4,3},{5,4},{6,5},{7,6},{8,7},{9,8},{10,9},{11,1... | collective-permute-start | bytes 786440 | tf_op jit(solution)/shard_map/ppermute | solution.py:27
  85.5 71.3 %reduce-scatter.9.cloned.1.call-start = ((), (), s32[]{:S(2)}) async-start(), calls=%async_computation.19 | async-start | bytes 655360 | tf_op jit(solution)/shard_map/reduce_scatter | solution.py:107
  133.6 30.5 %collective-permute-start.2 = (f32[256,256]{1,0:T(8,128)}, f32[256,256]{1,0:T(8,128)S(1)}, u32[]{:S(2)}, u32[]{:S(2)}) collective-permute-start(f32[256,256]{1,0:T(8,128)} %get-tuple-element.29), channel_id=1, source_target_pairs={{0,1},{1,2},{2,3},{3,4},{4,5},{5,6},{6,7},{7,8},{8,9},{9,10},{10,1... | collective-permute-start | bytes 786440 | tf_op jit(solution)/shard_map/ppermute | solution.py:24
  135.4 28.8 %collective-permute-start.3 = (f32[256,256]{1,0:T(8,128)}, f32[256,256]{1,0:T(8,128)}, u32[]{:S(2)}, u32[]{:S(2)}) collective-permute-start(f32[256,256]{1,0:T(8,128)} %get-tuple-element.30), channel_id=1, source_target_pairs={{1,0},{2,1},{3,2},{4,3},{5,4},{6,5},{7,6},{8,7},{9,8},{10,9},{11,1... | collective-permute-start | bytes 786440 | tf_op jit(solution)/shard_map/ppermute | solution.py:27
  159.5 16.3 %all-to-all-start.3 = ((f32[32,8,256]{2,1,0:T(8,128)}), f32[32,8,256]{2,1,0:T(8,128)S(1)}, u32[]{:S(2)}, u32[]{:S(2)}) async-start(f32[32,8,256]{2,1,0:T(8,128)} %bitcast.27), calls=%async_computation.5 | async-start | bytes 524288 | tf_op jit(solution)/shard_map/all_to_all | solution.py:110
  164.1 71.3 %reduce-scatter.11.cloned.1.call-start = ((), (), s32[]{:S(2)}) async-start(), calls=%async_computation.20 | async-start | bytes 655360 | tf_op jit(solution)/shard_map/reduce_scatter | solution.py:107
  212.3 30.5 %collective-permute-start.4 = (f32[256,256]{1,0:T(8,128)}, f32[256,256]{1,0:T(8,128)S(1)}, u32[]{:S(2)}, u32[]{:S(2)}) collective-permute-start(f32[256,256]{1,0:T(8,128)} %get-tuple-element.27), channel_id=1, source_target_pairs={{0,1},{1,2},{2,3},{3,4},{4,5},{5,6},{6,7},{7,8},{8,9},{9,10},{10,1... | collective-permute-start | bytes 786440 | tf_op jit(solution)/shard_map/ppermute | solution.py:24
  214.1 28.7 %collective-permute-start.5 = (f32[256,256]{1,0:T(8,128)}, f32[256,256]{1,0:T(8,128)}, u32[]{:S(2)}, u32[]{:S(2)}) collective-permute-start(f32[256,256]{1,0:T(8,128)} %get-tuple-element.28), channel_id=1, source_target_pairs={{1,0},{2,1},{3,2},{4,3},{5,4},{6,5},{7,6},{8,7},{9,8},{10,9},{11,1... | collective-permute-start | bytes 786440 | tf_op jit(solution)/shard_map/ppermute | solution.py:27
  238.2 16.2 %all-to-all-start.5 = ((f32[32,8,256]{2,1,0:T(8,128)}), f32[32,8,256]{2,1,0:T(8,128)S(1)}, u32[]{:S(2)}, u32[]{:S(2)}) async-start(f32[32,8,256]{2,1,0:T(8,128)} %bitcast.38), calls=%async_computation.8 | async-start | bytes 524288 | tf_op jit(solution)/shard_map/all_to_all | solution.py:110
  242.8 138.6 %reduce-scatter.13.cloned.1.call-start = ((), (), s32[]{:S(2)}) async-start(), calls=%async_computation.21 | async-start | bytes 655360 | tf_op jit(solution)/shard_map/reduce_scatter | solution.py:107
  358.2 30.5 %collective-permute-start.6 = (f32[256,256]{1,0:T(8,128)}, f32[256,256]{1,0:T(8,128)S(1)}, u32[]{:S(2)}, u32[]{:S(2)}) collective-permute-start(f32[256,256]{1,0:T(8,128)} %get-tuple-element.25), channel_id=1, source_target_pairs={{0,1},{1,2},{2,3},{3,4},{4,5},{5,6},{6,7},{7,8},{8,9},{9,10},{10,1... | collective-permute-start | bytes 786440 | tf_op jit(solution)/shard_map/ppermute | solution.py:24
  360.0 28.7 %collective-permute-start.7 = (f32[256,256]{1,0:T(8,128)}, f32[256,256]{1,0:T(8,128)}, u32[]{:S(2)}, u32[]{:S(2)}) collective-permute-start(f32[256,256]{1,0:T(8,128)} %get-tuple-element.26), channel_id=1, source_target_pairs={{1,0},{2,1},{3,2},{4,3},{5,4},{6,5},{7,6},{8,7},{9,8},{10,9},{11,1... | collective-permute-start | bytes 786440 | tf_op jit(solution)/shard_map/ppermute | solution.py:27
  384.0 16.2 %all-to-all-start.7 = ((f32[32,8,256]{2,1,0:T(8,128)}), f32[32,8,256]{2,1,0:T(8,128)S(1)}, u32[]{:S(2)}, u32[]{:S(2)}) async-start(f32[32,8,256]{2,1,0:T(8,128)} %bitcast.50), calls=%async_computation.11 | async-start | bytes 524288 | tf_op jit(solution)/shard_map/all_to_all | solution.py:110
  388.7 71.0 %reduce-scatter.15.cloned.1.call-start = ((), (), s32[]{:S(2)}) async-start(), calls=%async_computation.22 | async-start | bytes 655360 | tf_op jit(solution)/shard_map/reduce_scatter | solution.py:107
  436.5 30.7 %collective-permute-start.8 = (f32[256,256]{1,0:T(8,128)}, f32[256,256]{1,0:T(8,128)S(1)}, u32[]{:S(2)}, u32[]{:S(2)}) collective-permute-start(f32[256,256]{1,0:T(8,128)} %get-tuple-element.23), channel_id=1, source_target_pairs={{0,1},{1,2},{2,3},{3,4},{4,5},{5,6},{6,7},{7,8},{8,9},{9,10},{10,1... | collective-permute-start | bytes 786440 | tf_op jit(solution)/shard_map/ppermute | solution.py:24
  438.2 29.0 %collective-permute-start.9 = (f32[256,256]{1,0:T(8,128)}, f32[256,256]{1,0:T(8,128)}, u32[]{:S(2)}, u32[]{:S(2)}) collective-permute-start(f32[256,256]{1,0:T(8,128)} %get-tuple-element.24), channel_id=1, source_target_pairs={{1,0},{2,1},{3,2},{4,3},{5,4},{6,5},{7,6},{8,7},{9,8},{10,9},{11,1... | collective-permute-start | bytes 786440 | tf_op jit(solution)/shard_map/ppermute | solution.py:27
  462.3 16.4 %all-to-all-start.9 = ((f32[32,8,256]{2,1,0:T(8,128)}), f32[32,8,256]{2,1,0:T(8,128)S(1)}, u32[]{:S(2)}, u32[]{:S(2)}) async-start(f32[32,8,256]{2,1,0:T(8,128)} %bitcast.61), calls=%async_computation.14 | async-start | bytes 524288 | tf_op jit(solution)/shard_map/all_to_all | solution.py:110
  466.9 71.7 %reduce-scatter.17.cloned.1.call-start = ((), (), s32[]{:S(2)}) async-start(), calls=%async_computation.23 | async-start | bytes 655360 | tf_op jit(solution)/shard_map/reduce_scatter | solution.py:107
  514.4 31.1 %collective-permute-start.10 = (f32[256,256]{1,0:T(8,128)S(1)}, f32[256,256]{1,0:T(8,128)S(1)}, u32[]{:S(2)}, u32[]{:S(2)}) collective-permute-start(f32[256,256]{1,0:T(8,128)S(1)} %get-tuple-element.21), channel_id=1, source_target_pairs={{0,1},{1,2},{2,3},{3,4},{4,5},{5,6},{6,7},{7,8},{8,9},{9,10},{10,1... | collective-permute-start | bytes 786440 | tf_op jit(solution)/shard_map/ppermute | solution.py:24
  516.2 29.4 %collective-permute-start.11 = (f32[256,256]{1,0:T(8,128)S(1)}, f32[256,256]{1,0:T(8,128)S(1)}, u32[]{:S(2)}, u32[]{:S(2)}) collective-permute-start(f32[256,256]{1,0:T(8,128)S(1)} %get-tuple-element.22), channel_id=1, source_target_pairs={{1,0},{2,1},{3,2},{4,3},{5,4},{6,5},{7,6},{8,7},{9,8},{10,9},{11,1... | collective-permute-start | bytes 786440 | tf_op jit(solution)/shard_map/ppermute | solution.py:27
  541.3 15.7 %all-to-all-start.11 = ((f32[32,8,256]{2,1,0:T(8,128)}), f32[32,8,256]{2,1,0:T(8,128)S(1)}, u32[]{:S(2)}, u32[]{:S(2)}) async-start(f32[32,8,256]{2,1,0:T(8,128)} %bitcast.72), calls=%async_computation.17 | async-start | bytes 524288 | tf_op jit(solution)/shard_map/all_to_all | solution.py:110
  (6 other events, 180.0 us)
Sparse Core Ops, SparseCore 0:
  60.1 19.7 reduce-scatter.6
  131.9 24.8 reduce-scatter.8
  210.5 24.8 reduce-scatter.10
  356.4 24.8 reduce-scatter.12
  434.7 24.8 reduce-scatter.14
  513.5 25.0 reduce-scatter.16
